TPU v7x, 32 devices: a whole 2x2x4 slice. The times are simulated.
32 devices in a mesh: boson: 8 (over z, x), block: 4 (over y, core).
Axes of the slice: x: 2, y: 2, z: 4, core: 2. Of those that a mesh axis runs over, the one named last changes fastest.
Arguments:
- gamma_ph: bfloat16 [32, 1024, 1024], P('boson', 'block'), may hold values from -6 to 6
- full_ph: bfloat16 [32, 1024, 1024], P('boson', 'block'), may hold values from -0.1875 to 0.1875
- chi_ph: float32 [32, 1024], P('boson'), may hold values from 0.3 to 3
- pp_vertex: bfloat16 [32, 1024, 1024], P('boson', 'block'), may hold values from -0.1875 to 0.1875
- chi_pp: float32 [32, 1024], P('boson'), may hold values from 0.3 to 3
- relabel: int32 [32, 16, 8], replicated, may hold values from 0 to 31, as said below
Outputs:
- vertex_new: bfloat16 [32, 1024, 1024], P('boson', 'block')
Inputs may be any that keep to these rules, and one draw needn't show every extreme that they name: `relabel`: for each row tile and column block the table is a permutation of the 32 points. The owner of the target point (target // 4) is the source's owner (q // 4) plus a shift modulo 8, and both this shift and the target's position among its owner's points (target % 4) depend only on the row tile, the column block and q % 4. Row tiles b * 4 to (b + 1) * 4 - 1 form row block b; within one row block, at most 17 of the 128 triples of position, row tile and column block share a shift, and some shift is shared by exactly 17; in every row block the shifts 1, 4 and 7 each occur.
All inputs are finite; a program needn't handle non-finite values.
Results may differ from a plain program's by a relative error of at most 0.0063.
Values may be sent and summed in bfloat16 or wider, within the bound.
A program may use at most 128 MiB of HBM per device.

v0:
```python
import jax
import jax.numpy as jnp
from jax import lax
from jax.sharding import PartitionSpec as P

CB = 8
RS = 4


def to_tiles(matrix):
    points, row_count, order_size = matrix.shape
    tile_width = order_size // CB
    tile_rows = row_count // RS
    return (
        matrix.reshape(points, RS, tile_rows, CB, tile_width)
        .transpose(0, 1, 3, 2, 4)
        .reshape(points * RS * CB, tile_rows, tile_width)
    )


def from_tiles(tile_stack, points):
    total_tiles, tile_rows, tile_width = tile_stack.shape
    return (
        tile_stack.reshape(points, RS, CB, tile_rows, tile_width)
        .transpose(0, 1, 3, 2, 4)
        .reshape(points, RS * tile_rows, CB * tile_width)
    )


def scale_columns(left_side, column_scale):
    return (left_side.astype(jnp.float32) * column_scale[:, None, :]).astype(jnp.bfloat16)


def product_adder(scaled, shard_piece):
    return jnp.einsum("qij,qjk->qik", scaled, shard_piece, preferred_element_type=jnp.float32)


def pack_slots(tile_stack, slot_of_item, slot_total):
    item_total = tile_stack.shape[0]
    matches = (slot_of_item[None, :] == jnp.arange(slot_total, dtype=jnp.int32)[:, None]).astype(
        jnp.int32
    )
    item_index = jnp.sum(matches * jnp.arange(item_total, dtype=jnp.int32)[None, :], axis=1)
    filled = jnp.sum(matches, axis=1).astype(tile_stack.dtype)
    return jnp.take(tile_stack, item_index, axis=0) * filled[:, None, None]


def local(gamma_ph, full_ph, chi_ph, pp_vertex, chi_pp, relabel):
    points = gamma_ph.shape[0]
    nboson = lax.axis_size("boson")
    boson_here = lax.axis_index("boson")
    block_here = lax.axis_index("block")
    item_total = points * RS * CB
    capacity = -(-item_total // nboson) + 1
    phi_ph = product_adder(
        scale_columns(gamma_ph, chi_ph), lax.all_gather(full_ph, "block", axis=1, tiled=True)
    )
    ph_tiles = to_tiles(phi_ph.astype(jnp.bfloat16))
    tile_shape = ph_tiles.shape[1:]
    own_targets = lax.dynamic_slice(
        relabel, (boson_here * points, block_here * RS, 0), (points, RS, CB)
    ).reshape(item_total)
    shifts = (own_targets // points - boson_here) % nboson
    item_range = jnp.arange(item_total, dtype=jnp.int32)
    target = own_targets % points * (RS * CB) + item_range % (RS * CB)
    gather_order = jnp.sum(
        (target[None, :] == item_range[:, None]).astype(jnp.int32) * item_range[None, :], axis=1
    )
    earlier = (shifts[None, :] == shifts[:, None]) & (item_range[None, :] < item_range[:, None])
    slot_rank = jnp.sum(earlier.astype(jnp.int32), axis=1)
    send_slot = (boson_here + shifts) % nboson * capacity + slot_rank
    recv_slot = (boson_here - shifts) % nboson * capacity + slot_rank
    outgoing = pack_slots(ph_tiles, send_slot, nboson * capacity).reshape(
        (nboson, capacity) + tile_shape
    )
    incoming = lax.all_to_all(outgoing, "boson", split_axis=0, concat_axis=0, tiled=True).reshape(
        (nboson * capacity,) + tile_shape
    )
    arrived = jnp.take(incoming, recv_slot, axis=0)
    relabelled = from_tiles(jnp.take(arrived, gather_order, axis=0), points)
    phi_pp = product_adder(
        scale_columns(relabelled, chi_pp), lax.all_gather(pp_vertex, "block", axis=1, tiled=True)
    ).astype(jnp.bfloat16)
    leaving = jnp.take(to_tiles(phi_pp), target, axis=0)
    outgoing_back = pack_slots(leaving, recv_slot, nboson * capacity).reshape(
        (nboson, capacity) + tile_shape
    )
    incoming_back = lax.all_to_all(
        outgoing_back, "boson", split_axis=0, concat_axis=0, tiled=True
    ).reshape((nboson * capacity,) + tile_shape)
    returned = jnp.take(incoming_back, send_slot, axis=0)
    output = (
        gamma_ph.astype(jnp.float32) + phi_ph + from_tiles(returned, points).astype(jnp.float32)
    )
    return output.astype(jnp.bfloat16)


def solution(mesh):
    placed = (
        P("boson", "block", None),
        P("boson", "block", None),
        P("boson", None),
        P("boson", "block", None),
        P("boson", None),
        P(),
    )
    return jax.shard_map(
        local, mesh=mesh, in_specs=placed, out_specs=P("boson", "block", None), check_vma=False
    )
```

profile of v0, /device:TPU:0, one launch (start us, length us, event | category | flops | bytes accessed | tf_op | source)
XLA Modules:
  0.0 260.7 jit_solution(9437787763903134914)
XLA Ops:
  8.8 61.1 %all-gather.3.cloned.1.call-done = bf16[4,1024,1024]{2,1,0:T(8,128)(2,1)} async-done(((bf16[4,256,1024]{2,1,0:T(8,128)(2,1)}), bf16[4,1024,1024]{2,1,0:T(8,128)(2,1)}) %all-gather.3.cloned.1.call-update) | async-done | bytes 8388624 | tf_op jit(solution)/shard_map/all_gather | solution.py:56
  69.9 7.7 %fusion.22 = (bf16[4,256,1024]{2,1,0:T(8,128)(2,1)S(1)}, f32[4,256,1024]{2,1,0:T(8,128)}) fusion(bf16[4,1024,1024]{2,1,0:T(8,128)(2,1)} %all-gather.3.cloned.1.call-done, bf16[4,256,1024]{2,1,0:T(8,128)(2,1)S(1)} %copy-done.2, f32[4,1024]{1,0:T(4,128)S(1)} %copy-done.4), kind=kOutput, calls=%fused_computation.79 | convolution fusion | flops 2151677952 | bytes 16793600 | tf_op jit(solution)/shard_map/qij,qjk->qik/dot_general | solution.py:35
  78.8 2.4 gather_fusion
  81.3 3.5 %select_multiply_fusion.1 = bf16[136,64,128]{2,1,0:T(8,128)(2,1)} fusion(bf16[136,64,128]{2,1,0:T(8,128)(2,1)} %gather_fusion, pred[136]{0:T(512)(128)(4,1)S(1)} %compare_and_fusion.5, bf16[136]{0:T(256)(128)(2,1)S(1)} %convert_element_type.72), kind=kLoop, calls=%fused_computation.15 | loop fusion | flops 2228224 | bytes 4456856 | tf_op jit(solution)/shard_map/mul | solution.py:45
  84.8 5.3 %all-to-all-start = ((bf16[8,17,64,128]{3,2,1,0:T(8,128)(2,1)}), bf16[8,17,64,128]{3,2,1,0:T(8,128)(2,1)S(1)}, u32[]{:S(2)}, u32[]{:S(2)}) async-start(bf16[8,17,64,128]{3,2,1,0:T(8,128)(2,1)} %bitcast.2), calls=%async_computation | async-start | bytes 4456448 | tf_op jit(solution)/shard_map/all_to_all | solution.py:76
  90.3 51.2 %all-to-all-done = bf16[8,17,64,128]{3,2,1,0:T(8,128)(2,1)S(1)} async-done(((bf16[8,17,64,128]{3,2,1,0:T(8,128)(2,1)}), bf16[8,17,64,128]{3,2,1,0:T(8,128)(2,1)S(1)}, u32[]{:S(2)}, u32[]{:S(2)}) %all-to-all-start) | async-done | bytes 2228256 | tf_op jit(solution)/shard_map/all_to_all | solution.py:76
  141.6 2.1 gather_fusion.1
  143.7 1.9 broadcast_select_fusion.3
  145.6 2.1 gather_fusion.2
  147.7 1.9 broadcast_select_fusion.2
  150.1 5.2 %copy.19 = f32[4,4,64,8,128]{4,3,2,1,0:T(8,128)} copy(f32[4,4,64,8,128]{4,2,3,1,0:T(8,128)S(1)} %convert_bitcast_fusion.1) | data formatting | bytes 8388608 | tf_op jit(solution)/shard_map/convert_element_type | solution.py:31
  155.3 4.9 %reshape.233 = f32[4,256,1024]{2,1,0:T(8,128)} reshape(f32[4,4,64,8,128]{4,3,2,1,0:T(8,128)} %copy.19) | data formatting | bytes 8388608 | tf_op jit(solution)/shard_map/convert_element_type | solution.py:31
  160.2 7.0 %fusion.8 = bf16[4,256,1024]{2,1,0:T(8,128)(2,1)S(1)} fusion(bf16[4,1024,1024]{2,1,0:T(8,128)(2,1)} %all-gather.5.cloned.1.call-done, f32[4,256,1024]{2,1,0:T(8,128)} %reshape.233, f32[4,1024]{1,0:T(4,128)S(1)} %copy-done.5), kind=kOutput, calls=%fused_computation.24 | convolution fusion | flops 2150629376 | bytes 14696448 | tf_op jit(solution)/shard_map/qij,qjk->qik/dot_general | solution.py:35
  168.4 2.1 gather_fusion.3
  170.6 1.9 broadcast_select_fusion.1
  172.4 2.4 gather_fusion.4
  174.8 3.2 %select_multiply_fusion = bf16[136,64,128]{2,1,0:T(8,128)(2,1)} fusion(bf16[136,64,128]{2,1,0:T(8,128)(2,1)} %gather_fusion.4, pred[136]{0:T(512)(128)(4,1)S(1)} %compare_and_fusion.1, bf16[136]{0:T(256)(128)(2,1)S(1)} %convert_element_type.80), kind=kLoop, calls=%fused_computation.14 | loop fusion | flops 2228224 | bytes 4456856 | tf_op jit(solution)/shard_map/mul | solution.py:45
  178.0 3.8 %all-to-all-start.1 = ((bf16[8,17,64,128]{3,2,1,0:T(8,128)(2,1)}), bf16[8,17,64,128]{3,2,1,0:T(8,128)(2,1)S(1)}, u32[]{:S(2)}, u32[]{:S(2)}) async-start(bf16[8,17,64,128]{3,2,1,0:T(8,128)(2,1)} %bitcast.8), calls=%async_computation.1 | async-start | bytes 4456448 | tf_op jit(solution)/shard_map/all_to_all | solution.py:88
  181.9 51.1 %all-to-all-done.1 = bf16[8,17,64,128]{3,2,1,0:T(8,128)(2,1)S(1)} async-done(((bf16[8,17,64,128]{3,2,1,0:T(8,128)(2,1)}), bf16[8,17,64,128]{3,2,1,0:T(8,128)(2,1)S(1)}, u32[]{:S(2)}, u32[]{:S(2)}) %all-to-all-start.1) | async-done | bytes 2228256 | tf_op jit(solution)/shard_map/all_to_all | solution.py:88
  233.0 2.1 gather_fusion.5
  235.1 1.9 broadcast_select_fusion
  237.4 5.3 %copy.21 = f32[4,4,64,8,128]{4,3,2,1,0:T(8,128)} copy(f32[4,4,64,8,128]{4,2,3,1,0:T(8,128)S(1)} %convert_bitcast_fusion) | data formatting | bytes 8388608 | tf_op jit(solution)/shard_map/convert_element_type | solution.py:93
  242.7 5.0 %reshape.234 = f32[4,256,1024]{2,1,0:T(8,128)} reshape(f32[4,4,64,8,128]{4,3,2,1,0:T(8,128)} %copy.21) | data formatting | bytes 8388608 | tf_op jit(solution)/shard_map/convert_element_type | solution.py:93
  247.7 6.1 %fusion.2 = bf16[4,256,1024]{2,1,0:T(8,128)(2,1)} fusion(f32[4,256,1024]{2,1,0:T(8,128)} %reshape.234, f32[4,256,1024]{2,1,0:T(8,128)} %get-tuple-element.21, bf16[4,256,1024]{2,1,0:T(8,128)(2,1)S(1)} %copy-done.3), kind=kLoop, calls=%fused_computation.10 | loop fusion | flops 4194304 | bytes 12582912 | tf_op jit(solution)/shard_map/convert_element_type | solution.py:95
  (49 shorter events, 5.8 us)
Async XLA Ops:
  6.5 1.5 copy-start
  6.5 63.4 %copy-start.2 = (bf16[4,256,1024]{2,1,0:T(8,128)(2,1)S(1)}, bf16[4,256,1024]{2,1,0:T(8,128)(2,1)}, u32[]{:S(2)}) copy-start(bf16[4,256,1024]{2,1,0:T(8,128)(2,1)} %param.12) | copy-start | bytes 6291460
  6.5 63.4 %copy-start.4 = (f32[4,1024]{1,0:T(4,128)S(1)}, f32[4,1024]{1,0:T(4,128)}, u32[]{:S(2)}) copy-start(f32[4,1024]{1,0:T(4,128)} %param.14) | copy-start | bytes 49156
  6.5 63.4 %all-gather.3.cloned.1.call-start = ((), (), s32[]{:S(2)}) async-start(), calls=%async_computation.2 | async-start | bytes 10485760 | tf_op jit(solution)/shard_map/all_gather | solution.py:56
  7.3 152.9 %all-gather.5.cloned.1.call-start = ((), (), s32[]{:S(2)}) async-start(), calls=%async_computation.3 | async-start | bytes 10485760 | tf_op jit(solution)/shard_map/all_gather | solution.py:82
  84.8 56.8 %all-to-all-start = ((bf16[8,17,64,128]{3,2,1,0:T(8,128)(2,1)}), bf16[8,17,64,128]{3,2,1,0:T(8,128)(2,1)S(1)}, u32[]{:S(2)}, u32[]{:S(2)}) async-start(bf16[8,17,64,128]{3,2,1,0:T(8,128)(2,1)} %bitcast.2), calls=%async_computation | async-start | bytes 4456448 | tf_op jit(solution)/shard_map/all_to_all | solution.py:76
  155.3 4.9 %copy-start.5 = (f32[4,1024]{1,0:T(4,128)S(1)}, f32[4,1024]{1,0:T(4,128)}, u32[]{:S(2)}) copy-start(f32[4,1024]{1,0:T(4,128)} %param.16) | copy-start | bytes 49156
  178.0 54.9 %all-to-all-start.1 = ((bf16[8,17,64,128]{3,2,1,0:T(8,128)(2,1)}), bf16[8,17,64,128]{3,2,1,0:T(8,128)(2,1)S(1)}, u32[]{:S(2)}, u32[]{:S(2)}) async-start(bf16[8,17,64,128]{3,2,1,0:T(8,128)(2,1)} %bitcast.8), calls=%async_computation.1 | async-start | bytes 4456448 | tf_op jit(solution)/shard_map/all_to_all | solution.py:88
  242.7 5.0 %copy-start.3 = (bf16[4,256,1024]{2,1,0:T(8,128)(2,1)S(1)}, bf16[4,256,1024]{2,1,0:T(8,128)(2,1)}, u32[]{:S(2)}) copy-start(bf16[4,256,1024]{2,1,0:T(8,128)(2,1)} %param.12) | copy-start | bytes 6291460
  247.7 6.1 %copy-start.1 = (s32[32,16,8]{0,2,1:T(8,128)S(1)}, s32[32,16,8]{0,2,1:T(8,128)}, u32[]{:S(2)}) copy-start(s32[32,16,8]{0,2,1:T(8,128)} %param.17) | copy-start | bytes 49156
Sparse Core Ops, SparseCore 0:
  8.9 60.9 all-gather.2
  71.5 58.2 all-gather.4
where the time goes:
time: 261 us
  waiting for transfers between devices  165 us (63%)
  local copies, waits for them, and re-layouts  36.5 us (14%)
  other arithmetic  21.8 us (8%)
  matrix products  14.7 us (6%)
  between operations  13.7 us (5%)
  starting transfers between devices  9.13 us (3%)
    all_gather x1, waiting for transfers between devices, local(): lax.all_gather(full_ph, 'block', axis=1, tiled=True)  61.1 us
    all_to_all x1, waiting for transfers between devices, local(): lax.all_to_all(outgoing, 'boson', split_axis=0, concat_axis=0, tiled=True)  51.2 us
    all_to_all x1, waiting for transfers between devices, local(): lax.all_to_all(outgoing_back, 'boson', split_axis=0, concat_axis=0, tiled...  51.1 us
    dot_general x2, matrix products, product_adder(): jnp.einsum('qij,qjk->qik', scaled, shard_piece, preferred_element_type=jn...  14.7 us
    convert_element_type x2, local copies, waits for them, and re-layouts, local(): from_tiles(returned, points).astype(jnp.float32)  10.3 us
    convert_element_type x2, local copies, waits for them, and re-layouts, scale_columns(): left_side.astype(jnp.float32) * column_scale[:, None, :]  10.1 us
    mul x2, other arithmetic, pack_slots(): return jnp.take(tile_stack, item_index, axis=0) * filled[:, None, None]  6.72 us
    convert_element_type x1, other arithmetic, local(): return output.astype(jnp.bfloat16)  6.07 us
  transfers between devices with their start and end apart: 4, of which 3 were waited for; matrix products, arithmetic and copies ran while one was open for 13% of the time, Pallas kernels for 0%

commit v1 on v0

--- a/solution.py
+++ b/solution.py
@@ -53,7 +53,10 @@
     item_total = points * RS * CB
     capacity = -(-item_total // nboson) + 1
     phi_ph = product_adder(
-        scale_columns(gamma_ph, chi_ph), lax.all_gather(full_ph, "block", axis=1, tiled=True)
+        scale_columns(gamma_ph, chi_ph),
+        jnp.concatenate(
+            lax.all_to_all(jnp.stack([full_ph] * lax.axis_size("block")), "block", 0, 0), axis=1
+        ),
     )
     ph_tiles = to_tiles(phi_ph.astype(jnp.bfloat16))
     tile_shape = ph_tiles.shape[1:]

time: 261 us -> 357 us (1.37)
  waiting for transfers between devices: 165 us -> 241 us
  local copies, waits for them, and re-layouts: 36.5 us -> 49.9 us
  starting transfers between devices: 9.13 us -> 16.1 us
    all_to_all x0 -> x1, waiting for transfers between devices: none -> 138 us  [local(): lax.all_to_all(jnp.stack([full_ph] * lax.axis_size('block')), 'block', 0, 0)]
    all_gather x1 -> x0, waiting for transfers between devices: 61.1 us -> none  [local(): lax.all_gather(full_ph, 'block', axis=1, tiled=True)]
    reshape x0 -> x1, local copies, waits for them, and re-layouts: none -> 8.1 us  [local(): jnp.concatenate(lax.all_to_all(jnp.stack([full_ph] * lax.axis_size('block...]
    all_to_all x0 -> x1, starting transfers between devices: none -> 5.67 us  [local(): lax.all_to_all(jnp.stack([full_ph] * lax.axis_size('block')), 'block', 0, 0)]
    another operation x0 -> x1, local copies, waits for them, and re-layouts: none -> 4.37 us  [local(): jnp.stack([full_ph] * lax.axis_size('block'))]
where the time goes in v1:
time: 357 us; the launch traced here: 356 us
  waiting for transfers between devices  241 us (68%)
  local copies, waits for them, and re-layouts  49.9 us (14%)
  other arithmetic  21.5 us (6%)
  starting transfers between devices  16.1 us (5%)
  matrix products  14.7 us (4%)
  between operations  13.7 us (4%)
    all_to_all x1, waiting for transfers between devices, local(): lax.all_to_all(jnp.stack([full_ph] * lax.axis_size('block')), 'block', 0, 0)  138 us
    all_to_all x1, waiting for transfers between devices, local(): lax.all_to_all(outgoing_back, 'boson', split_axis=0, concat_axis=0, tiled...  51.1 us
    all_to_all x1, waiting for transfers between devices, local(): lax.all_to_all(outgoing, 'boson', split_axis=0, concat_axis=0, tiled=True)  50.9 us
    dot_general x2, matrix products, product_adder(): jnp.einsum('qij,qjk->qik', scaled, shard_piece, preferred_element_type=jn...  14.7 us
    convert_element_type x2, local copies, waits for them, and re-layouts, local(): from_tiles(returned, points).astype(jnp.float32)  10.3 us
    convert_element_type x2, local copies, waits for them, and re-layouts, scale_columns(): left_side.astype(jnp.float32) * column_scale[:, None, :]  10.1 us
    reshape x1, local copies, waits for them, and re-layouts, local(): jnp.concatenate(lax.all_to_all(jnp.stack([full_ph] * lax.axis_size('block...  8.1 us
  transfers between devices with their start and end apart: 4, of which 3 were waited for; matrix products, arithmetic and copies ran while one was open for 13% of the time, Pallas kernels for 0%

profile of v1, /device:TPU:0, one launch (start us, length us, event | category | flops | bytes accessed | tf_op | source)
XLA Modules:
  0.0 356.4 jit_solution(3400193529500774403)
XLA Ops:
  8.2 4.4 %stack.2 = bf16[4,4,256,1024]{3,2,1,0:T(8,128)(2,1)} broadcast(bf16[4,256,1024]{2,1,0:T(8,128)(2,1)S(1)} %copy-done.4), dimensions={1,2,3} | broadcast | bytes 10485760 | tf_op jit(solution)/shard_map/stack | solution.py:58
  12.5 5.7 %all-to-all-start = ((bf16[4,4,256,1024]{3,2,1,0:T(8,128)(2,1)}), bf16[4,4,256,1024]{3,2,1,0:T(8,128)(2,1)}, u32[]{:S(2)}, u32[]{:S(2)}) async-start(bf16[4,4,256,1024]{3,2,1,0:T(8,128)(2,1)} %stack.2), calls=%async_computation | async-start | bytes 16777216 | tf_op jit(solution)/shard_map/all_to_all | solution.py:58
  19.0 137.9 %all-to-all-done = bf16[4,4,256,1024]{3,2,1,0:T(8,128)(2,1)} async-done(((bf16[4,4,256,1024]{3,2,1,0:T(8,128)(2,1)}), bf16[4,4,256,1024]{3,2,1,0:T(8,128)(2,1)}, u32[]{:S(2)}, u32[]{:S(2)}) %all-to-all-start) | async-done | bytes 8388640 | tf_op jit(solution)/shard_map/all_to_all | solution.py:58
  156.9 8.1 %copy.23 = bf16[4,4,256,1024]{3,2,1,0:T(8,128)(2,1)} copy(bf16[4,4,256,1024]{3,2,0,1:T(8,128)(2,1)} %bitcast) | data formatting | bytes 16777216 | tf_op jit(solution)/shard_map/reshape | solution.py:57
  165.0 7.7 %fusion.22 = (bf16[4,256,1024]{2,1,0:T(8,128)(2,1)S(1)}, f32[4,256,1024]{2,1,0:T(8,128)}) fusion(bf16[4,1024,1024]{2,1,0:T(8,128)(2,1)} %bitcast.34, bf16[4,256,1024]{2,1,0:T(8,128)(2,1)S(1)} %copy-done.2, f32[4,1024]{1,0:T(4,128)S(1)} %copy-done.5), kind=kOutput, calls=%fused_computation.79 | convolution fusion | flops 2151677952 | bytes 16793600 | tf_op jit(solution)/shard_map/qij,qjk->qik/dot_general | solution.py:35
  174.0 2.4 gather_fusion
  176.4 3.2 select_multiply_fusion.1
  179.6 6.6 %all-to-all-start.1 = ((bf16[8,17,64,128]{3,2,1,0:T(8,128)(2,1)}), bf16[8,17,64,128]{3,2,1,0:T(8,128)(2,1)S(1)}, u32[]{:S(2)}, u32[]{:S(2)}) async-start(bf16[8,17,64,128]{3,2,1,0:T(8,128)(2,1)} %bitcast.4), calls=%async_computation.1 | async-start | bytes 4456448 | tf_op jit(solution)/shard_map/all_to_all | solution.py:79
  186.5 50.9 %all-to-all-done.1 = bf16[8,17,64,128]{3,2,1,0:T(8,128)(2,1)S(1)} async-done(((bf16[8,17,64,128]{3,2,1,0:T(8,128)(2,1)}), bf16[8,17,64,128]{3,2,1,0:T(8,128)(2,1)S(1)}, u32[]{:S(2)}, u32[]{:S(2)}) %all-to-all-start.1) | async-done | bytes 2228256 | tf_op jit(solution)/shard_map/all_to_all | solution.py:79
  237.3 2.1 gather_fusion.1
  239.5 1.9 broadcast_select_fusion.3
  241.3 2.1 gather_fusion.2
  245.8 5.2 %copy.26 = f32[4,4,64,8,128]{4,3,2,1,0:T(8,128)} copy(f32[4,4,64,8,128]{4,2,3,1,0:T(8,128)S(1)} %convert_bitcast_fusion.1) | data formatting | bytes 8388608 | tf_op jit(solution)/shard_map/convert_element_type | solution.py:31
  251.0 4.9 %reshape.243 = f32[4,256,1024]{2,1,0:T(8,128)} reshape(f32[4,4,64,8,128]{4,3,2,1,0:T(8,128)} %copy.26) | data formatting | bytes 8388608 | tf_op jit(solution)/shard_map/convert_element_type | solution.py:31
  255.9 7.0 %fusion.8 = bf16[4,256,1024]{2,1,0:T(8,128)(2,1)S(1)} fusion(bf16[4,1024,1024]{2,1,0:T(8,128)(2,1)} %all-gather.2.cloned.1.call-done, f32[4,256,1024]{2,1,0:T(8,128)} %reshape.243, f32[4,1024]{1,0:T(4,128)S(1)} %copy-done.6), kind=kOutput, calls=%fused_computation.24 | convolution fusion | flops 2150629376 | bytes 14696448 | tf_op jit(solution)/shard_map/qij,qjk->qik/dot_general | solution.py:35
  264.2 2.1 gather_fusion.3
  268.2 2.4 gather_fusion.4
  270.6 3.2 select_multiply_fusion
  273.8 3.8 %all-to-all-start.2 = ((bf16[8,17,64,128]{3,2,1,0:T(8,128)(2,1)}), bf16[8,17,64,128]{3,2,1,0:T(8,128)(2,1)S(1)}, u32[]{:S(2)}, u32[]{:S(2)}) async-start(bf16[8,17,64,128]{3,2,1,0:T(8,128)(2,1)} %bitcast.10), calls=%async_computation.2 | async-start | bytes 4456448 | tf_op jit(solution)/shard_map/all_to_all | solution.py:91
  277.6 51.1 %all-to-all-done.2 = bf16[8,17,64,128]{3,2,1,0:T(8,128)(2,1)S(1)} async-done(((bf16[8,17,64,128]{3,2,1,0:T(8,128)(2,1)}), bf16[8,17,64,128]{3,2,1,0:T(8,128)(2,1)S(1)}, u32[]{:S(2)}, u32[]{:S(2)}) %all-to-all-start.2) | async-done | bytes 2228256 | tf_op jit(solution)/shard_map/all_to_all | solution.py:91
  328.7 2.1 gather_fusion.5
  333.2 5.3 %copy.28 = f32[4,4,64,8,128]{4,3,2,1,0:T(8,128)} copy(f32[4,4,64,8,128]{4,2,3,1,0:T(8,128)S(1)} %convert_bitcast_fusion) | data formatting | bytes 8388608 | tf_op jit(solution)/shard_map/convert_element_type | solution.py:96
  338.5 5.0 %reshape.244 = f32[4,256,1024]{2,1,0:T(8,128)} reshape(f32[4,4,64,8,128]{4,3,2,1,0:T(8,128)} %copy.28) | data formatting | bytes 8388608 | tf_op jit(solution)/shard_map/convert_element_type | solution.py:96
  343.5 6.1 %fusion.2 = bf16[4,256,1024]{2,1,0:T(8,128)(2,1)} fusion(f32[4,256,1024]{2,1,0:T(8,128)} %reshape.244, f32[4,256,1024]{2,1,0:T(8,128)} %get-tuple-element.21, bf16[4,256,1024]{2,1,0:T(8,128)(2,1)S(1)} %copy-done.3), kind=kLoop, calls=%fused_computation.10 | loop fusion | flops 4194304 | bytes 12582912 | tf_op jit(solution)/shard_map/convert_element_type | solution.py:98
  (52 shorter events, 11.6 us)
Async XLA Ops:
  6.5 11.7 %copy-start = (s32[32,16,8]{0,2,1:T(8,128)S(1)}, s32[32,16,8]{0,2,1:T(8,128)}, u32[]{:S(2)}) copy-start(s32[32,16,8]{0,2,1:T(8,128)} %param.17) | copy-start | bytes 49156
  6.5 1.6 copy-start.4
  6.5 249.4 %all-gather.2.cloned.1.call-start = ((), (), s32[]{:S(2)}) async-start(), calls=%async_computation.3 | async-start | bytes 10485760 | tf_op jit(solution)/shard_map/all_gather | solution.py:85
  12.5 144.4 %all-to-all-start = ((bf16[4,4,256,1024]{3,2,1,0:T(8,128)(2,1)}), bf16[4,4,256,1024]{3,2,1,0:T(8,128)(2,1)}, u32[]{:S(2)}, u32[]{:S(2)}) async-start(bf16[4,4,256,1024]{3,2,1,0:T(8,128)(2,1)} %stack.2), calls=%async_computation | async-start | bytes 16777216 | tf_op jit(solution)/shard_map/all_to_all | solution.py:58
  156.9 8.1 %copy-start.2 = (bf16[4,256,1024]{2,1,0:T(8,128)(2,1)S(1)}, bf16[4,256,1024]{2,1,0:T(8,128)(2,1)}, u32[]{:S(2)}) copy-start(bf16[4,256,1024]{2,1,0:T(8,128)(2,1)} %param.12) | copy-start | bytes 6291460
  156.9 8.1 %copy-start.5 = (f32[4,1024]{1,0:T(4,128)S(1)}, f32[4,1024]{1,0:T(4,128)}, u32[]{:S(2)}) copy-start(f32[4,1024]{1,0:T(4,128)} %param.14) | copy-start | bytes 49156
  179.6 57.8 %all-to-all-start.1 = ((bf16[8,17,64,128]{3,2,1,0:T(8,128)(2,1)}), bf16[8,17,64,128]{3,2,1,0:T(8,128)(2,1)S(1)}, u32[]{:S(2)}, u32[]{:S(2)}) async-start(bf16[8,17,64,128]{3,2,1,0:T(8,128)(2,1)} %bitcast.4), calls=%async_computation.1 | async-start | bytes 4456448 | tf_op jit(solution)/shard_map/all_to_all | solution.py:79
  251.0 4.9 %copy-start.6 = (f32[4,1024]{1,0:T(4,128)S(1)}, f32[4,1024]{1,0:T(4,128)}, u32[]{:S(2)}) copy-start(f32[4,1024]{1,0:T(4,128)} %param.16) | copy-start | bytes 49156
  273.8 54.9 %all-to-all-start.2 = ((bf16[8,17,64,128]{3,2,1,0:T(8,128)(2,1)}), bf16[8,17,64,128]{3,2,1,0:T(8,128)(2,1)S(1)}, u32[]{:S(2)}, u32[]{:S(2)}) async-start(bf16[8,17,64,128]{3,2,1,0:T(8,128)(2,1)} %bitcast.10), calls=%async_computation.2 | async-start | bytes 4456448 | tf_op jit(solution)/shard_map/all_to_all | solution.py:91
  338.5 5.0 %copy-start.3 = (bf16[4,256,1024]{2,1,0:T(8,128)(2,1)S(1)}, bf16[4,256,1024]{2,1,0:T(8,128)(2,1)}, u32[]{:S(2)}) copy-start(bf16[4,256,1024]{2,1,0:T(8,128)(2,1)} %param.12) | copy-start | bytes 6291460
  343.5 6.1 %copy-start.1 = (s32[32,16,8]{0,2,1:T(8,128)S(1)}, s32[32,16,8]{0,2,1:T(8,128)}, u32[]{:S(2)}) copy-start(s32[32,16,8]{0,2,1:T(8,128)} %param.17) | copy-start | bytes 49156
Sparse Core Ops, SparseCore 0:
  8.9 106.0 all-gather.1
